TPU v7x, 32 devices: a whole 2x2x4 slice. The times are simulated.
32 devices in a mesh: tower: 2 (over core), batch: 16 (over z, y, x).
Axes of the slice: x: 2, y: 2, z: 4, core: 2. Of those that a mesh axis runs over, the one named last changes fastest.
Arguments:
- tokens: bfloat16 [2, 32768, 768], P('tower', 'batch'), may hold values from -6 to 6
- lengths: int32 [2, 64], P('tower', 'batch'), may hold values from 64 to 512, as said below
- prefixes: int32 [2, 64], P('tower', 'batch'), may hold values from 1 to 32
- positives: int32 [64], replicated, may hold values from 0 to 63, each once
- gain_attention: float32 [768], replicated, may hold values from 0.5 to 1.5
- query_weight: bfloat16 [768, 768], replicated, may hold values from -0.02734375 to 0.02734375
- key_weight: bfloat16 [768, 768], replicated, may hold values from -0.21875 to 0.21875
- value_weight: bfloat16 [768, 768], replicated, may hold values from -0.21875 to 0.21875
- output_weight: bfloat16 [768, 768], replicated, may hold values from -1.75 to 1.75
- bucket_bias: float32 [32, 12], replicated, may hold values from -4 to 4
- gain_feedforward: float32 [768], replicated, may hold values from 0.5 to 1.5
- widen_weight: bfloat16 [768, 3072], replicated, may hold values from -0.21875 to 0.21875
- narrow_weight: bfloat16 [3072, 768], replicated, may hold values from -0.109375 to 0.109375
- gain_final: float32 [768], replicated, may hold values from 0.5 to 1.5
Outputs:
- contrast_loss: float32 [], replicated
- score_gradient: float32 [64, 64], P('batch')
- token_gradient: bfloat16 [2, 32768, 768], P('tower', 'batch')
- grad_attention: float32 [768], replicated
- grad_query: float32 [768, 768], replicated
- grad_key: float32 [768, 768], replicated
- grad_value: float32 [768, 768], replicated
- grad_output: float32 [768, 768], replicated
- grad_bucket: float32 [32, 12], replicated
- grad_feedforward: float32 [768], replicated
- grad_widen: float32 [768, 3072], replicated
- grad_narrow: float32 [3072, 768], replicated
- grad_final: float32 [768], replicated
Inputs may be any that keep to these rules, and one draw needn't show every extreme that they name: `lengths`: sequence 0 of each side uses all 512 positions. `positives`: every document is the positive of exactly one query.
All inputs are finite; a program needn't handle non-finite values.
Results may differ from a plain program's by a relative error of at most 0.025.
The roundings to bfloat16 on the way count: a program that leaves them out, or rounds other values in their place, can miss the bound.
Values sent between devices are 32-bit elements; how exact they have to be, the bound alone decides.
A program may use at most 320 MiB of HBM per device.

v0:
```python
import jax
import jax.numpy as jnp
from jax import lax
from jax.sharding import PartitionSpec as P

epsilon = 1e-06
masked_score = -1000000000.0
score_scale = 100.0
far_steps = (12, 16, 23, 32, 46, 64, 91)
highest = lax.Precision.HIGHEST


def bucket_onehot(slot_len, bucket_count):
    places = jnp.arange(slot_len, dtype=jnp.int32)
    offset = places[None, :] - places[:, None]
    spread = jnp.abs(offset)
    far_bucket = 8 + sum(((spread >= step).astype(jnp.int32) for step in far_steps))
    bucket = jnp.where(spread < 8, spread, far_bucket) + jnp.where(
        offset > 0, bucket_count // 2, 0
    ).astype(jnp.int32)
    labels = jnp.arange(bucket_count, dtype=jnp.int32)
    return (bucket[:, :, None] == labels[None, None, :]).astype(jnp.float32)


def norm_forward(values, scale_vec):
    inverse = lax.rsqrt(jnp.mean(values * values, axis=-1, keepdims=True) + epsilon)
    return (values * inverse * scale_vec, inverse)


def norm_backward(values, inverse, scale_vec, upstream):
    scaled = upstream * scale_vec
    inner_mean = jnp.mean(scaled * values, axis=-1, keepdims=True)
    grad_values = inverse * scaled - values * (inverse * inverse * inverse) * inner_mean
    grad_scale = jnp.sum(upstream * values * inverse, axis=0)
    return (grad_values, grad_scale)


def local(
    tokens,
    lengths,
    prefixes,
    positives,
    gain_attention,
    query_weight,
    key_weight,
    value_weight,
    output_weight,
    bucket_bias,
    gain_feedforward,
    widen_weight,
    narrow_weight,
    gain_final,
):
    seqs = lengths.shape[1]
    rows = tokens.shape[1]
    slot_len = rows // seqs
    width = tokens.shape[2]
    heads = bucket_bias.shape[1]
    head_dim = query_weight.shape[1] // heads
    inner = heads * head_dim
    tokens_f = tokens[0].astype(jnp.float32)
    seq_lengths = lengths[0]
    seq_prefix = prefixes[0]
    onehot = bucket_onehot(slot_len, bucket_bias.shape[0])
    bias = jnp.einsum("ijb,bh->hij", onehot, bucket_bias, precision=highest)
    normed_f, inverse_first = norm_forward(tokens_f, gain_attention)
    normed = normed_f.astype(jnp.bfloat16)

    def project(matrix):
        projected = jnp.dot(normed, matrix, preferred_element_type=jnp.float32).astype(jnp.bfloat16)
        return projected.reshape(seqs, slot_len, heads, head_dim)

    query_all = project(query_weight)
    key_all = project(key_weight)
    value_all = project(value_weight)
    places = jnp.arange(slot_len, dtype=jnp.int32)
    valid = places[None, :] < seq_lengths[:, None]

    def score_block(query_rows, key_rows, valid_keys):
        raw_scores = jnp.einsum(
            "ihd,jhd->hij", query_rows, key_rows, preferred_element_type=jnp.float32
        )
        return jnp.where(valid_keys[None, None, :], raw_scores + bias, masked_score)

    def attend_forward(parts):
        query_rows, key_rows, value_rows, valid_keys = parts
        scores = score_block(query_rows, key_rows, valid_keys)
        row_peak = jnp.max(scores, axis=-1, keepdims=True)
        raised = jnp.exp(scores - row_peak)
        totals = jnp.sum(raised, axis=-1, keepdims=True)
        soft_low = (raised / totals).astype(jnp.bfloat16)
        context = jnp.einsum(
            "hij,jhd->ihd", soft_low, value_rows, preferred_element_type=jnp.float32
        )
        return (context.astype(jnp.bfloat16), (row_peak + jnp.log(totals))[:, :, 0])

    context, log_totals = lax.map(attend_forward, (query_all, key_all, value_all, valid))
    context_flat = context.reshape(rows, inner)
    mixed = tokens_f + jnp.dot(context_flat, output_weight, preferred_element_type=jnp.float32)
    ffn_in_f, inverse_second = norm_forward(mixed, gain_feedforward)
    ffn_in = ffn_in_f.astype(jnp.bfloat16)
    pre_act = jnp.dot(ffn_in, widen_weight, preferred_element_type=jnp.float32)
    hidden = jnp.where(pre_act > 0, pre_act, 0.0).astype(jnp.bfloat16)
    output = mixed + jnp.dot(hidden, narrow_weight, preferred_element_type=jnp.float32)
    final, inverse_third = norm_forward(output, gain_final)
    pool_mask = ((places[None, :] >= seq_prefix[:, None]) & valid).astype(jnp.float32)
    pool_weight = pool_mask / jnp.sum(pool_mask, axis=1, keepdims=True)
    pooled = jnp.sum(final.reshape(seqs, slot_len, width) * pool_weight[:, :, None], axis=1)
    inverse_pool = lax.rsqrt(jnp.sum(pooled * pooled, axis=-1, keepdims=True) + epsilon)
    unit = pooled * inverse_pool
    gathered = lax.all_gather(unit, ("tower", "batch"), axis=0, tiled=True)
    total_seqs = gathered.shape[0] // 2
    query_units = gathered[:total_seqs]
    doc_units = gathered[total_seqs:]
    scores = score_scale * jnp.dot(query_units, doc_units.T, precision=highest)
    labels = jnp.arange(total_seqs, dtype=jnp.int32)
    target = (positives[:, None] == labels[None, :]).astype(jnp.float32)
    row_peak = jnp.max(scores, axis=1, keepdims=True)
    row_raised = jnp.exp(scores - row_peak)
    row_sum = jnp.sum(row_raised, axis=1, keepdims=True)
    col_peak = jnp.max(scores, axis=0, keepdims=True)
    col_raised = jnp.exp(scores - col_peak)
    col_sum = jnp.sum(col_raised, axis=0, keepdims=True)
    loss_value = (
        0.5 * jnp.sum(row_peak[:, 0] + jnp.log(row_sum[:, 0]))
        + 0.5 * jnp.sum(col_peak[0] + jnp.log(col_sum[0]))
        - jnp.sum(target * scores)
    )
    score_grad = 0.5 * row_raised / row_sum + 0.5 * col_raised / col_sum - target
    tower = lax.axis_index("tower")
    first_row = lax.axis_index("batch") * seqs
    my_rows = lax.dynamic_slice_in_dim(score_grad, first_row, seqs, 0)
    my_cols = lax.dynamic_slice_in_dim(score_grad, first_row, seqs, 1)
    grad_as_query = score_scale * jnp.dot(my_rows, doc_units, precision=highest)
    grad_as_doc = score_scale * jnp.dot(my_cols.T, query_units, precision=highest)
    grad_unit = jnp.where(tower == 0, grad_as_query, grad_as_doc)
    cubed = inverse_pool * inverse_pool * inverse_pool
    grad_pooled = inverse_pool * grad_unit - pooled * cubed * jnp.sum(
        grad_unit * pooled, axis=-1, keepdims=True
    )
    grad_fin = (pool_weight[:, :, None] * grad_pooled[:, None, :]).reshape(rows, width)
    grad_out, grad_final = norm_backward(output, inverse_third, gain_final, grad_fin)
    grad_branch = grad_out.astype(jnp.bfloat16)
    grad_narrow = jnp.einsum("tf,td->fd", hidden, grad_branch, preferred_element_type=jnp.float32)
    grad_hidden = jnp.einsum(
        "td,fd->tf", grad_branch, narrow_weight, preferred_element_type=jnp.float32
    )
    grad_pre = jnp.where(pre_act > 0, grad_hidden, 0.0).astype(jnp.bfloat16)
    grad_widen = jnp.einsum("td,tf->df", ffn_in, grad_pre, preferred_element_type=jnp.float32)
    grad_ffn_in = jnp.einsum(
        "tf,df->td", grad_pre, widen_weight, preferred_element_type=jnp.float32
    )
    grad_mixed_norm, grad_feedforward = norm_backward(
        mixed, inverse_second, gain_feedforward, grad_ffn_in
    )
    grad_mixed = grad_out + grad_mixed_norm
    grad_attn = grad_mixed.astype(jnp.bfloat16)
    grad_output = jnp.einsum(
        "ti,td->id", context_flat, grad_attn, preferred_element_type=jnp.float32
    )
    grad_context = jnp.einsum(
        "td,id->ti", grad_attn, output_weight, preferred_element_type=jnp.float32
    )
    grad_context = grad_context.astype(jnp.bfloat16).reshape(seqs, slot_len, heads, head_dim)

    def attend_backward(bias_total, parts):
        query_rows, key_rows, value_rows, valid_keys, log_rows, context_grad = parts
        scores_here = score_block(query_rows, key_rows, valid_keys)
        soft = jnp.exp(scores_here - log_rows[:, :, None])
        soft_low = soft.astype(jnp.bfloat16)
        value_part = jnp.einsum(
            "hij,ihd->jhd", soft_low, context_grad, preferred_element_type=jnp.float32
        )
        grad_soft = jnp.einsum(
            "ihd,jhd->hij", context_grad, value_rows, preferred_element_type=jnp.float32
        )
        grad_scores = soft * (grad_soft - jnp.sum(grad_soft * soft, axis=-1, keepdims=True))
        scores_low = grad_scores.astype(jnp.bfloat16)
        query_part = jnp.einsum(
            "hij,jhd->ihd", scores_low, key_rows, preferred_element_type=jnp.float32
        )
        key_part = jnp.einsum(
            "hij,ihd->jhd", scores_low, query_rows, preferred_element_type=jnp.float32
        )
        return (
            bias_total + grad_scores,
            (
                query_part.astype(jnp.bfloat16),
                key_part.astype(jnp.bfloat16),
                value_part.astype(jnp.bfloat16),
            ),
        )

    bias_total, (query_grads, key_grads, value_grads) = lax.scan(
        attend_backward,
        jnp.zeros(bias.shape, jnp.float32),
        (query_all, key_all, value_all, valid, log_totals, grad_context),
    )
    query_grads = query_grads.reshape(rows, inner)
    key_grads = key_grads.reshape(rows, inner)
    value_grads = value_grads.reshape(rows, inner)
    grad_bucket = jnp.einsum("ijb,hij->bh", onehot, bias_total, precision=highest)
    grad_query = jnp.einsum("td,ti->di", normed, query_grads, preferred_element_type=jnp.float32)
    grad_key = jnp.einsum("td,ti->di", normed, key_grads, preferred_element_type=jnp.float32)
    grad_value = jnp.einsum("td,ti->di", normed, value_grads, preferred_element_type=jnp.float32)
    grad_normed = (
        jnp.einsum("ti,di->td", query_grads, query_weight, preferred_element_type=jnp.float32)
        + jnp.einsum("ti,di->td", key_grads, key_weight, preferred_element_type=jnp.float32)
        + jnp.einsum("ti,di->td", value_grads, value_weight, preferred_element_type=jnp.float32)
    )
    grad_tokens_norm, grad_attention = norm_backward(
        tokens_f, inverse_first, gain_attention, grad_normed
    )
    token_gradient = (grad_mixed + grad_tokens_norm).astype(jnp.bfloat16)[None]
    (
        sum_attention,
        sum_query,
        sum_key,
        sum_value,
        sum_output,
        sum_bucket,
        sum_feedforward,
        sum_widen,
        sum_narrow,
        sum_final,
    ) = lax.psum(
        (
            grad_attention,
            grad_query,
            grad_key,
            grad_value,
            grad_output,
            grad_bucket,
            grad_feedforward,
            grad_widen,
            grad_narrow,
            grad_final,
        ),
        ("tower", "batch"),
    )
    return (
        loss_value,
        my_rows,
        token_gradient,
        sum_attention,
        sum_query,
        sum_key,
        sum_value,
        sum_output,
        sum_bucket,
        sum_feedforward,
        sum_widen,
        sum_narrow,
        sum_final,
    )


def solution(mesh):
    placed = (
        P("tower", "batch", None),
        P("tower", "batch"),
        P("tower", "batch"),
        P(),
        P(),
        P(),
        P(),
        P(),
        P(),
        P(),
        P(),
        P(),
        P(),
        P(),
    )
    return jax.shard_map(
        local,
        mesh=mesh,
        in_specs=placed,
        out_specs=(
            P(),
            P("batch", None),
            P("tower", "batch", None),
            P(),
            P(),
            P(),
            P(),
            P(),
            P(),
            P(),
            P(),
            P(),
            P(),
        ),
        check_vma=False,
    )
```

profile of v0, /device:TPU:0, one launch (start us, length us, event | category | flops | bytes accessed | tf_op | source)
XLA Modules:
  0.0 1078.6 jit_solution(5208512605683882147)
XLA Ops:
  13.9 6.6 convolution_convert_fusion.4
  20.5 4.9 copy.68
  25.4 6.2 reshape.320
  31.7 4.4 copy.71
  40.2 4.6 copy.69
  44.8 6.1 reshape.321
  51.0 4.4 copy.72
  59.5 4.6 copy.67
  64.1 6.2 reshape.319
  70.2 4.3 copy.70
  74.6 13.7 %fusion.55 = f32[12,512,512]{2,0,1:T(8,128)} fusion(s32[512,512]{1,0:T(8,128)S(1)} %fusion.93, f32[32,12]{0,1:T(8,128)S(1)} %copy-done.36), kind=kOutput, calls=%fused_computation.65 | convolution fusion | flops 1216348160 | bytes 13633024 | tf_op jit(solution)/shard_map/ijb,bh->hij/dot_general | solution.py:65
  88.2 17.3 %copy.73 = f32[12,512,512]{1,2,0:T(8,128)} copy(f32[12,512,512]{2,0,1:T(8,128)} %fusion.55) | data formatting | bytes 25165824 | tf_op jit(solution)/shard_map/while | solution.py:97
  107.6 59.8 %while.29 = (s32[]{:T(128)}, bf16[4,512,12,64]{1,3,2,0:T(8,128)(2,1)}, f32[4,12,512]{2,1,0:T(8,128)}, bf16[4,512,12,64]{1,3,2,0:T(8,128)(2,1)}, pred[4,512]{1,0:...) while((s32[]{:T(128)}, ...), condition=%wide.region_4.5_spmd, body=%wide.region_1.4_spmd.sunk | while | flops 830859264 | bytes 53685868 | solution.py:97
  108.2 8.0 fusion.177
  117.9 4.4 fusion.179
  123.0 8.0 fusion.177
  132.7 4.4 fusion.179
  137.7 8.0 fusion.177
  147.5 4.4 fusion.179
  152.5 8.0 fusion.177
  162.3 4.4 fusion.179
  167.4 4.5 copy.74
  179.0 13.7 %fusion.113 = f32[2048,3072]{1,0:T(8,128)} fusion(bf16[768,3072]{1,0:T(8,128)(2,1)S(1)} %bitcast.270, f32[2048,768]{1,0:T(8,128)S(1)} %get-tuple-element.306, f32[768]{0:T(1024)S(1)} %copy-done.46, f32[2048]{0:T(1024)S(1)} %get-tuple-element.298), kind=kOutput, calls=%fused_computation.170 | convolution fusion | flops 9668395008 | bytes 36187136 | tf_op jit(solution)/shard_map/dot_general | solution.py:102
  192.7 19.2 %multiply_reduce_fusion.4 = (f32[2048]{0:T(1024)S(1)}, f32[2048,768]{1,0:T(8,128)}) fusion(f32[2048,768]{1,0:T(8,128)} %copy-done.16, bf16[3072,768]{1,0:T(8,128)(2,1)} %param.30, f32[2048,3072]{1,0:T(8,128)} %fusion.113), kind=kOutput, calls=%fused_computation.101 | convolution fusion | flops 9687267328 | bytes 42475520 | tf_op jit(solution)/shard_map/dot_general | solution.py:104
  215.5 72.1 %all-gather = f32[32,4,768]{2,1,0:T(4,128)S(1)} all-gather(f32[1,4,768]{2,1,0:T(4,128)S(1)} %multiply_bitcast_fusion), channel_id=1, replica_groups=mesh['tower'=2,'batch'=16] {'tower','batch'}, dimensions={0}, use_global_device_ids=true | all-gather | bytes 405504 | tf_op jit(solution)/shard_map/all_gather | solution.py:111
  290.5 4.8 fusion.81
  295.3 4.9 fusion.82
  300.3 18.3 %fusion.83 = f32[3072,768]{1,0:T(8,128)} fusion(bf16[2048,768]{1,0:T(8,128)(2,1)} %fusion.82, f32[2048,3072]{1,0:T(8,128)} %fusion.113), kind=kOutput, calls=%fused_computation.110 | convolution fusion | flops 9682550784 | bytes 37748736 | tf_op jit(solution)/shard_map/tf,td->fd/dot_general | solution.py:144
  318.5 20.8 %fusion.52 = bf16[2048,3072]{1,0:T(8,128)(2,1)} fusion(f32[2048,3072]{1,0:T(8,128)} %fusion.113, bf16[2048,768]{1,0:T(8,128)(2,1)} %fusion.82, bf16[3072,768]{1,0:T(8,128)(2,1)} %param.30), kind=kOutput, calls=%fused_computation.62 | convolution fusion | flops 9682550784 | bytes 45613056 | tf_op jit(solution)/shard_map/td,fd->tf/dot_general | solution.py:145
  339.4 17.4 %multiply_reduce_fusion.1 = (f32[768]{0:T(1024)}, f32[2048]{0:T(1024)S(1)}, f32[2048,768]{1,0:T(8,128)}) fusion(f32[2048,768]{1,0:T(8,128)S(1)} %bitcast.254, f32[2048]{0:T(1024)S(1)} %get-tuple-element.298, f32[768]{0:T(1024)S(1)} %copy-done.46, bf16[2048,3072]{1,0:T(8,128)(2,1)} %fusion.52, bf16[768,3072]{1,0:T(8,128)(2,1)} %param.29), kind=kOutput, calls=%fused_computation.95 | convolution fusion | flops 9673110528 | bytes 29906944 | tf_op jit(solution)/shard_map/tf,df->td/dot_general | solution.py:150
  356.8 15.6 %fusion.112 = f32[768,3072]{1,0:T(8,128)} fusion(bf16[2048,3072]{1,0:T(8,128)(2,1)} %fusion.52, f32[2048,768]{1,0:T(8,128)S(1)} %bitcast.254, f32[768]{0:T(1024)S(1)} %copy-done.46, f32[2048]{0:T(1024)S(1)} %get-tuple-element.298), kind=kOutput, calls=%fused_computation.169 | convolution fusion | flops 9668395008 | bytes 28322816 | tf_op jit(solution)/shard_map/td,tf->df/dot_general | solution.py:149
  384.0 4.7 copy.75
  388.8 6.5 reshape.324
  395.3 4.3 copy.79
  405.7 183.0 %while.30 = (s32[]{:T(128)}, f32[12,512,512]{1,2,0:T(8,128)}, bf16[4,512,12,64]{1,3,2,0:T(8,128)(2,1)}, bf16[4,512,12,64]{1,3,2,0:T(8,128)(2,1)}, bf16[4,512,12,...) while((s32[]{:T(128)}, f32[12,512,512]{1,2,0:T(8,128)}, ...), condition=%wide.region_22.23_spmd.clone, body=%wide.region_20.22_spmd.clone.sunk | while | flops 2049042432 | bytes 177863392 | solution.py:194
  406.5 8.8 subtract_exponential_fusion.5
  418.3 7.5 multiply_reduce_fusion.9
  425.8 13.5 %fusion.188 = (bf16[12,512,512]{1,2,0:T(8,128)(2,1)}, f32[12,512,512]{1,2,0:T(8,128)}) fusion(f32[12,512,512]{1,2,0:T(8,128)S(1)} %subtract_exponential_fusion.5, f32[12,512,512]{1,2,0:T(8,128)} %get-tuple-element.446, f32[12,512]{1,0:T(8,128)S(1)} %get-tuple-element.447, f32[12,512,512]{1,2,0:T(8,128)} %get-tuple-element.492, pred[]{:T(512)S(6)} %compare.3), kind=kLoop, calls=%fused_computation.24.clone.1 | loop fusion | flops 15728640 | bytes 56647680 | tf_op jit(solution)/shard_map/while/body/eval_jaxpr/convert_element_type | solution.py:178
  439.3 6.1 fusion.190
  449.3 8.8 subtract_exponential_fusion.5
  461.1 7.5 multiply_reduce_fusion.9
  468.6 17.4 %fusion.188 = (bf16[12,512,512]{1,2,0:T(8,128)(2,1)}, f32[12,512,512]{1,2,0:T(8,128)}) fusion(f32[12,512,512]{1,2,0:T(8,128)S(1)} %subtract_exponential_fusion.5, f32[12,512,512]{1,2,0:T(8,128)} %get-tuple-element.446, f32[12,512]{1,0:T(8,128)S(1)} %get-tuple-element.447, f32[12,512,512]{1,2,0:T(8,128)} %get-tuple-element.492, pred[]{:T(512)S(6)} %compare.3), kind=kLoop, calls=%fused_computation.24.clone.1 | loop fusion | flops 15728640 | bytes 56647680 | tf_op jit(solution)/shard_map/while/body/eval_jaxpr/convert_element_type | solution.py:178
  486.0 6.1 fusion.190
  496.0 8.8 subtract_exponential_fusion.5
  507.8 7.5 multiply_reduce_fusion.9
  515.3 17.4 %fusion.188 = (bf16[12,512,512]{1,2,0:T(8,128)(2,1)}, f32[12,512,512]{1,2,0:T(8,128)}) fusion(f32[12,512,512]{1,2,0:T(8,128)S(1)} %subtract_exponential_fusion.5, f32[12,512,512]{1,2,0:T(8,128)} %get-tuple-element.446, f32[12,512]{1,0:T(8,128)S(1)} %get-tuple-element.447, f32[12,512,512]{1,2,0:T(8,128)} %get-tuple-element.492, pred[]{:T(512)S(6)} %compare.3), kind=kLoop, calls=%fused_computation.24.clone.1 | loop fusion | flops 15728640 | bytes 56647680 | tf_op jit(solution)/shard_map/while/body/eval_jaxpr/convert_element_type | solution.py:178
  532.7 6.1 fusion.190
  542.6 8.8 subtract_exponential_fusion.5
  554.4 7.5 multiply_reduce_fusion.9
  561.9 17.4 %fusion.188 = (bf16[12,512,512]{1,2,0:T(8,128)(2,1)}, f32[12,512,512]{1,2,0:T(8,128)}) fusion(f32[12,512,512]{1,2,0:T(8,128)S(1)} %subtract_exponential_fusion.5, f32[12,512,512]{1,2,0:T(8,128)} %get-tuple-element.446, f32[12,512]{1,0:T(8,128)S(1)} %get-tuple-element.447, f32[12,512,512]{1,2,0:T(8,128)} %get-tuple-element.492, pred[]{:T(512)S(6)} %compare.3), kind=kLoop, calls=%fused_computation.24.clone.1 | loop fusion | flops 15728640 | bytes 56647680 | tf_op jit(solution)/shard_map/while/body/eval_jaxpr/convert_element_type | solution.py:178
  579.3 6.1 fusion.190
  588.8 4.5 copy.83
  594.3 4.6 fusion.114
  602.5 5.1 fusion.118
  612.6 4.6 fusion.116
  617.3 18.7 %copy.84 = f32[12,512,512]{2,0,1:T(8,128)} copy(f32[12,512,512]{1,2,0:T(8,128)} %get-tuple-element.126) | data formatting | bytes 25165824 | tf_op jit(solution)/shard_map/while | solution.py:194
  638.6 8.1 fusion.126
  646.6 7.9 fusion.127
  654.5 17.5 %fusion.92 = f32[32,12]{0,1:T(8,128)S(1)} fusion(f32[12,512,512]{2,0,1:T(8,128)S(1)} %copy-done.2, s32[512,512]{1,0:T(8,128)S(1)} %copy-done.11), kind=kOutput, calls=%fused_computation.121 | convolution fusion | flops 1216348160 | bytes 13633024 | tf_op jit(solution)/shard_map/ijb,hij->bh/dot_general | solution.py:202
  672.1 9.1 fusion.71
  681.2 39.6 %all-reduce = (f32[768]{0:T(1024)}, f32[32,12]{0,1:T(8,128)}, f32[768]{0:T(1024)}, f32[768]{0:T(1024)}) all-reduce(f32[768]{0:T(1024)S(1)} %get-tuple-element.228, f32[32,12]{0,1:T(8,128)S(1)} %fusion.92, f32[768]{0:T(1024)S(1)} %copy-done.47, f32[768]{0:T(1024)S(1)} %copy-done.33), channel_id=1, replica_groups=mesh['tower'=2,'batch'=16] {'tower','batch'}, use_global_device_ids=true, to_apply=%region_25.26 | all-reduce | flops 2688 | bytes 21504 | tf_op jit(solution)/shard_map/psum | solution.py:226
  720.8 8.3 fusion.87
  729.1 320.5 %all-reduce.4.cloned.1.call-done = (f32[768,768]{1,0:T(8,128)}, f32[768,768]{1,0:T(8,128)}, f32[768,768]{1,0:T(8,128)}, f32[768,768]{1,0:T(8,128)}, f32[768,3072]{1,0:T(8,128)}, /*index=5*/f32[3072,768]{1,0:T(8,128)}) async-done(((f32[768,768]{1,0:T(8,128)}, f32[768,768]{1,0:T(8,128)}, f32[768,768]{1,0:T(8,128)}, f32[768,768]{1,0:T(8,128)}, f32[768,3072]{1,0:T(8,128)}, /*index=5*/f32[3072,768]{1,0:T(8,128)}), ...) | async-done | bytes 28311568 | tf_op jit(solution)/shard_map/psum | solution.py:226
  1057.3 9.3 copy.133
  (220 shorter events, 106.9 us)
Async XLA Ops:
  7.2 48.2 %copy-start = (bf16[768,768]{1,0:T(8,128)(2,1)S(1)}, bf16[768,768]{1,0:T(8,128)(2,1)}, u32[]{:S(2)}) copy-start(bf16[768,768]{1,0:T(8,128)(2,1)} %param.25) | copy-start | bytes 3538948
  7.2 1042.5 %all-reduce.4.cloned.1.call-start = ((), (), s32[]{:S(2)}) async-start(), calls=%async_computation | async-start | bytes 56623104 | tf_op jit(solution)/shard_map/psum | solution.py:226
  7.7 66.9 %copy-start.10 = (s32[512,512]{1,0:T(8,128)}, s32[512,512]{1,0:T(8,128)S(1)}, u32[]{:S(2)}) copy-start(s32[512,512]{1,0:T(8,128)S(1)} %fusion.93) | copy-start | bytes 3145732
  12.5 42.9 %copy-start.27 = (f32[2048]{0:T(1024)}, f32[2048]{0:T(1024)S(1)}, u32[]{:S(2)}) copy-start(f32[2048]{0:T(1024)S(1)} %get-tuple-element.296) | copy-start | bytes 24580
  25.4 10.7 copy-start.34
  25.4 10.7 copy-start.52
  31.7 4.4 copy-start.4
  50.9 4.4 copy-start.5
  64.1 10.5 copy-start.36
  167.4 5.6 copy-start.25
  167.4 5.6 copy-start.6
  167.4 5.6 copy-start.49
  171.9 7.1 slice-start.7
  173.0 6.0 copy-start.46
  173.0 6.0 slice-start.8
  192.7 19.2 %copy-start.29 = (f32[768]{0:T(1024)S(1)}, f32[768]{0:T(1024)}, u32[]{:S(2)}) copy-start(f32[768]{0:T(1024)} %param.31) | copy-start | bytes 9220
  192.7 19.2 %copy-start.31 = (f32[4,512]{1,0:T(4,128)S(1)}, f32[4,512]{1,0:T(4,128)}, u32[]{:S(2)}) copy-start(f32[4,512]{1,0:T(4,128)} %get-tuple-element.302) | copy-start | bytes 24580
  211.9 76.4 %copy-start.48 = (s32[64]{0:T(128)S(1)}, s32[64]{0:T(128)}, u32[]{:S(2)}) copy-start(s32[64]{0:T(128)} %param.21) | copy-start | bytes 772
  211.9 78.2 %copy-start.32 = (f32[1,4,4,128]{3,2,1,0:T(4,128)S(1)}, f32[1,4,4,128]{3,2,1,0:T(4,128)}, u32[]{:S(2)}) copy-start(f32[1,4,4,128]{3,2,1,0:T(4,128)} %get-tuple-element.301) | copy-start | bytes 24580
  288.3 7.1 copy-start.37
  288.3 7.1 copy-start.39
  290.1 5.3 copy-start.41
  295.3 44.0 %slice-start.5 = ((s8[6291456]{0:T(1024)(128)(4,1)}), s8[4194304]{0:T(1024)(128)(4,1)S(1)}, s32[]{:S(2)}) async-start(s8[6291456]{0:T(1024)(128)(4,1)} %bitcast.253), calls=%async_computation.6 | async-start | bytes 8388608
  300.3 39.1 %slice-start.6 = ((s8[6291456]{0:T(1024)(128)(4,1)}), s8[2097152]{0:T(1024)(128)(4,1)S(1)}, s32[]{:S(2)}) async-start(s8[6291456]{0:T(1024)(128)(4,1)} %bitcast.253), calls=%async_computation.7 | async-start | bytes 4194304
  318.5 53.8 %slice-start = ((s8[6291456]{0:T(1024)(128)(4,1)}), s8[2097152]{0:T(1024)(128)(4,1)S(1)}, s32[]{:S(2)}) async-start(s8[6291456]{0:T(1024)(128)(4,1)} %bitcast.243), calls=%async_computation.1 | async-start | bytes 4194304
  339.4 33.0 %slice-start.1 = ((s8[6291456]{0:T(1024)(128)(4,1)}), s8[4194304]{0:T(1024)(128)(4,1)S(1)}, s32[]{:S(2)}) async-start(s8[6291456]{0:T(1024)(128)(4,1)} %bitcast.243), calls=%async_computation.2 | async-start | bytes 8388608
  356.8 15.6 %copy-start.17 = (f32[2048,768]{1,0:T(8,128)S(1)}, f32[2048,768]{1,0:T(8,128)}, u32[]{:S(2)}) copy-start(f32[2048,768]{1,0:T(8,128)} %get-tuple-element.312) | copy-start | bytes 18874372
  372.4 3.5 copy-start.19
  375.9 4.1 copy-start.9
  376.0 4.1 copy-start.50
  399.6 6.1 copy-start.26
  406.5 8.8 copy-start.3
  439.3 6.1 copy-start.1
  449.3 8.8 copy-start.3
  486.0 6.1 copy-start.1
  496.0 8.8 copy-start.3
  532.7 6.1 copy-start.1
  542.6 8.8 copy-start.3
  579.3 6.1 copy-start.1
  588.7 5.6 copy-start.7
  588.8 5.6 copy-start.28
  588.8 5.5 copy-start.35
  594.3 4.7 copy-start.14
  594.3 4.6 copy-start.13
  602.4 5.1 copy-start.20
  602.4 5.1 copy-start.12
  617.2 18.7 %copy-start.38 = (f32[64]{0:T(128)S(1)}, f32[64]{0:T(128)}, u32[]{:S(2)}) copy-start(f32[64]{0:T(128)} %copy-done.37) | copy-start | bytes 772
  617.2 18.7 %copy-start.40 = (f32[64]{0:T(128)S(1)}, f32[64]{0:T(128)}, u32[]{:S(2)}) copy-start(f32[64]{0:T(128)} %copy-done.39) | copy-start | bytes 772
  617.3 18.7 %copy-start.43 = (f32[64]{0:T(128)S(1)}, f32[64]{0:T(128)}, u32[]{:S(2)}) copy-start(f32[64]{0:T(128)} %copy-done.42) | copy-start | bytes 772
  617.3 18.7 %copy-start.45 = (f32[64]{0:T(128)S(1)}, f32[64]{0:T(128)}, u32[]{:S(2)}) copy-start(f32[64]{0:T(128)} %copy-done.44) | copy-start | bytes 772
  617.3 21.3 %copy-start.51 = (bf16[768,768]{1,0:T(8,128)(2,1)S(1)}, bf16[768,768]{1,0:T(8,128)(2,1)}, u32[]{:S(2)}) copy-start(bf16[768,768]{1,0:T(8,128)(2,1)} %param.23) | copy-start | bytes 3538948
  638.5 16.0 %copy-start.2 = (f32[12,512,512]{2,0,1:T(8,128)S(1)}, f32[12,512,512]{2,0,1:T(8,128)}, u32[]{:S(2)}) copy-start(f32[12,512,512]{2,0,1:T(8,128)} %copy.84) | copy-start | bytes 37748740
  646.6 7.9 copy-start.11
  654.5 17.5 %copy-start.8 = (bf16[1,2048,768]{2,1,0:T(8,128)(2,1)S(1)}, bf16[1,2048,768]{2,1,0:T(8,128)(2,1)}, u32[]{:S(2)}) copy-start(bf16[1,2048,768]{2,1,0:T(8,128)(2,1)} %param.18) | copy-start | bytes 9437188
  654.5 17.5 %copy-start.15 = (bf16[96,8,4,512]{3,1,2,0:T(8,128)(2,1)S(1)}, bf16[96,8,4,512]{3,1,2,0:T(8,128)(2,1)}, u32[]{:S(2)}) copy-start(bf16[96,8,4,512]{3,1,2,0:T(8,128)(2,1)} %copy-done.14) | copy-start | bytes 9437188
  672.1 9.1 copy-start.33
  672.1 9.1 copy-start.47
  672.1 48.7 %copy-start.30 = (f32[2048]{0:T(1024)S(1)}, f32[2048]{0:T(1024)}, u32[]{:S(2)}) copy-start(f32[2048]{0:T(1024)} %get-tuple-element.295) | copy-start | bytes 24580
  1049.7 3.4 copy-start.24
  1049.7 4.8 copy-start.23
  1049.7 6.2 copy-start.22
  1055.9 10.7 slice-start.2
  1057.3 9.3 slice-start.3
  1057.3 9.3 slice-start.4
  (5 other events, 8.8 us)
Sparse Core Ops, SparseCore 0:
  617.4 432.2 all-reduce.3
where the time goes:
time: 1080 us
  matrix products  366 us (34%)
  waiting for transfers between devices  321 us (30%)
  local copies, waits for them, and re-layouts  153 us (14%)
  blocking collectives  112 us (10%)
  other arithmetic  109 us (10%)
  between operations  18 us (2%)
    psum x1, waiting for transfers between devices, local(): lax.psum((grad_attention, grad_query, grad_key, grad_value, grad_output,...  321 us
    all_gather x1, blocking collectives, local(): gathered = lax.all_gather(unit, ('tower', 'batch'), axis=0, tiled=True)  72.1 us
    dot_general x8, matrix products, score_block(): jnp.einsum('ihd,jhd->hij', query_rows, key_rows, preferred_element_type=j...  67.1 us
    convert_element_type x4, other arithmetic, attend_backward(): scores_low = grad_scores.astype(jnp.bfloat16)  65.7 us
    psum x1, blocking collectives, local(): lax.psum((grad_attention, grad_query, grad_key, grad_value, grad_output,...  39.6 us
    while x5, local copies, waits for them, and re-layouts, local(): lax.map(attend_forward, (query_all, key_all, value_all, valid))  35 us
    unnamed x132, local copies, waits for them, and re-layouts  34.2 us
    dot_general x4, matrix products, attend_backward(): jnp.einsum('ihd,jhd->hij', context_grad, value_rows, preferred_element_ty...  30 us
  transfers between devices with their start and end apart: 1, of which 1 were waited for; matrix products, arithmetic and copies ran while one was open for 7% of the time, Pallas kernels for 0%

commit v1 on v0

--- a/solution.py
+++ b/solution.py
@@ -8,6 +8,11 @@
 score_scale = 100.0
 far_steps = (12, 16, 23, 32, 46, 64, 91)
 highest = lax.Precision.HIGHEST
+
+
+def axis_by_axis(array, axis_one, axis_two):
+    half = lax.psum(array, axis_one)
+    return lax.psum(half, axis_two)
 
 
 def bucket_onehot(slot_len, bucket_count):
@@ -223,7 +228,7 @@
         sum_widen,
         sum_narrow,
         sum_final,
-    ) = lax.psum(
+    ) = axis_by_axis(
         (
             grad_attention,
             grad_query,
@@ -236,7 +241,8 @@
             grad_narrow,
             grad_final,
         ),
-        ("tower", "batch"),
+        "batch",
+        "tower",
     )
     return (
         loss_value,

time: 1080 us -> 1560 us (1.44)
  waiting for transfers between devices: 321 us -> 748 us
  blocking collectives: 112 us -> 151 us
    psum x1 -> x2, waiting for transfers between devices: 321 us -> 748 us  [the longest x1 748 us: axis_by_axis(): half = lax.psum(array, axis_one)]
    psum x1 -> x2, blocking collectives: 39.6 us -> 79 us  [the longest x1 75 us: axis_by_axis(): half = lax.psum(array, axis_one)]
  transfers between devices with their start and end apart: 1 -> 2, of which waited for: 1 -> 1; matrix products, arithmetic and copies ran while one was open for 7% -> 5% of each run, Pallas kernels for 0% -> 0%
where the time goes in v1:
time: 1560 us; the launch traced here: 1550 us
  waiting for transfers between devices  748 us (48%)
  matrix products  370 us (24%)
  local copies, waits for them, and re-layouts  154 us (10%)
  blocking collectives  151 us (10%)
  other arithmetic  109 us (7%)
  between operations  18 us (1%)
    psum x1, waiting for transfers between devices, axis_by_axis(): half = lax.psum(array, axis_one)  748 us
    psum x1, blocking collectives, axis_by_axis(): half = lax.psum(array, axis_one)  75 us
    all_gather x1, blocking collectives, local(): gathered = lax.all_gather(unit, ('tower', 'batch'), axis=0, tiled=True)  72.1 us
    dot_general x8, matrix products, score_block(): jnp.einsum('ihd,jhd->hij', query_rows, key_rows, preferred_element_type=j...  67.1 us
    convert_element_type x4, other arithmetic, attend_backward(): scores_low = grad_scores.astype(jnp.bfloat16)  66.2 us
    while x5, local copies, waits for them, and re-layouts, local(): lax.map(attend_forward, (query_all, key_all, value_all, valid))  35.3 us
    unnamed x132, local copies, waits for them, and re-layouts  34.2 us
  transfers between devices with their start and end apart: 2, of which 1 were waited for; matrix products, arithmetic and copies ran while one was open for 5% of the time, Pallas kernels for 0%

profile of v1, /device:TPU:0, one launch (start us, length us, event | category | flops | bytes accessed | tf_op | source)
XLA Modules:
  0.0 1551.7 jit_solution(15842778743503892094)
XLA Ops:
  13.9 6.6 convolution_convert_fusion.4
  20.5 4.9 copy.68
  25.4 6.2 reshape.320
  31.6 4.5 copy.71
  40.2 4.6 copy.69
  44.8 6.1 reshape.321
  51.0 4.4 copy.72
  59.5 4.6 copy.67
  64.1 6.2 reshape.319
  70.3 4.3 copy.70
  74.6 13.7 fusion.55
  88.2 17.6 %copy.73 = f32[12,512,512]{1,2,0:T(8,128)} copy(f32[12,512,512]{2,0,1:T(8,128)} %fusion.55) | data formatting | bytes 25165824 | tf_op jit(solution)/shard_map/while | solution.py:102
  107.9 59.8 %while.29 = (s32[]{:T(128)}, bf16[4,512,12,64]{1,3,2,0:T(8,128)(2,1)}, f32[4,12,512]{2,1,0:T(8,128)}, bf16[4,512,12,64]{1,3,2,0:T(8,128)(2,1)}, pred[4,512]{1,0:...) while((s32[]{:T(128)}, ...), condition=%wide.region_4.5_spmd, body=%wide.region_1.4_spmd.sunk | while | flops 830859264 | bytes 53685868 | solution.py:102
  108.5 8.0 fusion.177
  118.2 4.4 fusion.179
  123.2 8.0 fusion.177
  133.0 4.4 fusion.179
  138.0 8.0 fusion.177
  147.8 4.4 fusion.179
  152.8 8.0 fusion.177
  162.5 4.4 fusion.179
  167.7 4.5 copy.74
  179.3 13.8 fusion.113
  193.1 19.2 %multiply_reduce_fusion.4 = (f32[2048]{0:T(1024)S(1)}, f32[2048,768]{1,0:T(8,128)}) fusion(f32[2048,768]{1,0:T(8,128)} %copy-done.16, bf16[3072,768]{1,0:T(8,128)(2,1)} %param.30, f32[2048,3072]{1,0:T(8,128)} %fusion.113), kind=kOutput, calls=%fused_computation.101 | convolution fusion | flops 9687267328 | bytes 42475520 | tf_op jit(solution)/shard_map/dot_general | solution.py:109
  215.9 72.1 %all-gather = f32[32,4,768]{2,1,0:T(4,128)S(1)} all-gather(f32[1,4,768]{2,1,0:T(4,128)S(1)} %multiply_bitcast_fusion), channel_id=1, replica_groups=mesh['tower'=2,'batch'=16] {'tower','batch'}, dimensions={0}, use_global_device_ids=true | all-gather | bytes 405504 | tf_op jit(solution)/shard_map/all_gather | solution.py:116
  290.9 4.8 fusion.81
  295.7 4.9 fusion.82
  300.6 18.3 %fusion.83 = f32[3072,768]{1,0:T(8,128)} fusion(bf16[2048,768]{1,0:T(8,128)(2,1)} %fusion.82, f32[2048,3072]{1,0:T(8,128)} %fusion.113), kind=kOutput, calls=%fused_computation.110 | convolution fusion | flops 9682550784 | bytes 37748736 | tf_op jit(solution)/shard_map/tf,td->fd/dot_general | solution.py:149
  318.9 21.0 %fusion.52 = bf16[2048,3072]{1,0:T(8,128)(2,1)} fusion(f32[2048,3072]{1,0:T(8,128)} %fusion.113, bf16[2048,768]{1,0:T(8,128)(2,1)} %fusion.82, bf16[3072,768]{1,0:T(8,128)(2,1)} %param.30), kind=kOutput, calls=%fused_computation.62 | convolution fusion | flops 9682550784 | bytes 45613056 | tf_op jit(solution)/shard_map/td,fd->tf/dot_general | solution.py:150
  339.9 17.4 %multiply_reduce_fusion.1 = (f32[768]{0:T(1024)}, f32[2048]{0:T(1024)S(1)}, f32[2048,768]{1,0:T(8,128)}) fusion(f32[2048,768]{1,0:T(8,128)S(1)} %bitcast.254, f32[2048]{0:T(1024)S(1)} %get-tuple-element.308, f32[768]{0:T(1024)S(1)} %copy-done.46, bf16[2048,3072]{1,0:T(8,128)(2,1)} %fusion.52, bf16[768,3072]{1,0:T(8,128)(2,1)} %param.29), kind=kOutput, calls=%fused_computation.95 | convolution fusion | flops 9673110528 | bytes 29906944 | tf_op jit(solution)/shard_map/tf,df->td/dot_general | solution.py:155
  357.3 15.6 %fusion.112 = f32[768,3072]{1,0:T(8,128)} fusion(bf16[2048,3072]{1,0:T(8,128)(2,1)} %fusion.52, f32[2048,768]{1,0:T(8,128)S(1)} %bitcast.254, f32[768]{0:T(1024)S(1)} %copy-done.46, f32[2048]{0:T(1024)S(1)} %get-tuple-element.308), kind=kOutput, calls=%fused_computation.169 | convolution fusion | flops 9668395008 | bytes 28322816 | tf_op jit(solution)/shard_map/td,tf->df/dot_general | solution.py:154
  384.6 4.7 copy.75
  389.3 6.5 reshape.324
  395.9 4.3 copy.79
  406.3 183.2 %while.30 = (s32[]{:T(128)}, f32[12,512,512]{1,2,0:T(8,128)}, bf16[4,512,12,64]{1,3,2,0:T(8,128)(2,1)}, bf16[4,512,12,64]{1,3,2,0:T(8,128)(2,1)}, bf16[4,512,12,...) while((s32[]{:T(128)}, f32[12,512,512]{1,2,0:T(8,128)}, ...), condition=%wide.region_22.23_spmd.clone, body=%wide.region_20.22_spmd.clone.sunk | while | flops 2049042432 | bytes 177863392 | solution.py:199
  407.1 8.8 subtract_exponential_fusion.5
  418.8 7.5 multiply_reduce_fusion.9
  426.3 13.6 fusion.188
  439.9 6.1 fusion.190
  449.9 8.8 subtract_exponential_fusion.5
  461.6 7.5 multiply_reduce_fusion.9
  469.1 17.5 %fusion.188 = (bf16[12,512,512]{1,2,0:T(8,128)(2,1)}, f32[12,512,512]{1,2,0:T(8,128)}) fusion(f32[12,512,512]{1,2,0:T(8,128)S(1)} %subtract_exponential_fusion.5, f32[12,512,512]{1,2,0:T(8,128)} %get-tuple-element.456, f32[12,512]{1,0:T(8,128)S(1)} %get-tuple-element.457, f32[12,512,512]{1,2,0:T(8,128)} %get-tuple-element.502, pred[]{:T(512)S(6)} %compare.3), kind=kLoop, calls=%fused_computation.24.clone.1 | loop fusion | flops 15728640 | bytes 56647680 | tf_op jit(solution)/shard_map/while/body/eval_jaxpr/convert_element_type | solution.py:183
  486.6 6.1 fusion.190
  496.7 8.8 subtract_exponential_fusion.5
  508.4 7.5 multiply_reduce_fusion.9
  515.9 17.5 %fusion.188 = (bf16[12,512,512]{1,2,0:T(8,128)(2,1)}, f32[12,512,512]{1,2,0:T(8,128)}) fusion(f32[12,512,512]{1,2,0:T(8,128)S(1)} %subtract_exponential_fusion.5, f32[12,512,512]{1,2,0:T(8,128)} %get-tuple-element.456, f32[12,512]{1,0:T(8,128)S(1)} %get-tuple-element.457, f32[12,512,512]{1,2,0:T(8,128)} %get-tuple-element.502, pred[]{:T(512)S(6)} %compare.3), kind=kLoop, calls=%fused_computation.24.clone.1 | loop fusion | flops 15728640 | bytes 56647680 | tf_op jit(solution)/shard_map/while/body/eval_jaxpr/convert_element_type | solution.py:183
  533.4 6.1 fusion.190
  543.4 8.8 subtract_exponential_fusion.5
  555.2 7.5 multiply_reduce_fusion.9
  562.7 17.5 %fusion.188 = (bf16[12,512,512]{1,2,0:T(8,128)(2,1)}, f32[12,512,512]{1,2,0:T(8,128)}) fusion(f32[12,512,512]{1,2,0:T(8,128)S(1)} %subtract_exponential_fusion.5, f32[12,512,512]{1,2,0:T(8,128)} %get-tuple-element.456, f32[12,512]{1,0:T(8,128)S(1)} %get-tuple-element.457, f32[12,512,512]{1,2,0:T(8,128)} %get-tuple-element.502, pred[]{:T(512)S(6)} %compare.3), kind=kLoop, calls=%fused_computation.24.clone.1 | loop fusion | flops 15728640 | bytes 56647680 | tf_op jit(solution)/shard_map/while/body/eval_jaxpr/convert_element_type | solution.py:183
  580.2 6.0 fusion.190
  589.6 4.5 copy.83
  595.1 4.6 fusion.114
  603.3 5.1 fusion.118
  613.5 4.6 fusion.116
  618.2 748.5 %all-reduce.7.cloned.1.call-done = (f32[768,768]{1,0:T(8,128)}, f32[768,768]{1,0:T(8,128)}, f32[768,768]{1,0:T(8,128)}, f32[768,768]{1,0:T(8,128)}, f32[768,3072]{1,0:T(8,128)}, /*index=5*/f32[3072,768]{1,0:T(8,128)}) async-done(((f32[768,768]{1,0:T(8,128)}, f32[768,768]{1,0:T(8,128)}, f32[768,768]{1,0:T(8,128)}, f32[768,768]{1,0:T(8,128)}, f32[768,3072]{1,0:T(8,128)}, /*index=5*/f32[3072,768]{1,0:T(8,128)}), ...) | async-done | bytes 28311568 | tf_op jit(solution)/shard_map/psum | solution.py:14
  1366.7 19.2 %copy.84 = f32[12,512,512]{2,0,1:T(8,128)} copy(f32[12,512,512]{1,2,0:T(8,128)} %get-tuple-element.126) | data formatting | bytes 25165824 | tf_op jit(solution)/shard_map/while | solution.py:199
  1388.5 9.1 fusion.126
  1397.7 10.3 fusion.127
  1408.0 17.5 %fusion.92 = f32[32,12]{0,1:T(8,128)S(1)} fusion(f32[12,512,512]{2,0,1:T(8,128)S(1)} %copy-done.2, s32[512,512]{1,0:T(8,128)S(1)} %copy-done.11), kind=kOutput, calls=%fused_computation.121 | convolution fusion | flops 1216348160 | bytes 13633024 | tf_op jit(solution)/shard_map/ijb,hij->bh/dot_general | solution.py:207
  1425.5 10.2 fusion.71
  1435.7 75.0 %all-reduce = (f32[768]{0:T(1024)S(1)}, f32[32,12]{0,1:T(8,128)S(1)}, f32[768]{0:T(1024)S(1)}, f32[768]{0:T(1024)S(1)}) all-reduce(f32[768]{0:T(1024)S(1)} %get-tuple-element.228, f32[32,12]{0,1:T(8,128)S(1)} %fusion.92, f32[768]{0:T(1024)S(1)} %copy-done.47, f32[768]{0:T(1024)S(1)} %copy-done.33), channel_id=1, replica_groups=mesh['tower'=2,'batch'=16] {'batch'}, use_global_device_ids=true, to_apply=%region_25.26 | all-reduce | flops 2688 | bytes 21504 | tf_op jit(solution)/shard_map/psum | solution.py:14
  1514.7 8.1 fusion.87
  1530.5 9.3 copy.139
  (224 shorter events, 110.9 us)
Async XLA Ops:
  7.2 48.2 %copy-start = (bf16[768,768]{1,0:T(8,128)(2,1)S(1)}, bf16[768,768]{1,0:T(8,128)(2,1)}, u32[]{:S(2)}) copy-start(bf16[768,768]{1,0:T(8,128)(2,1)} %param.25) | copy-start | bytes 3538948
  7.2 1359.4 %all-reduce.7.cloned.1.call-start = ((), (), s32[]{:S(2)}) async-start(), calls=%async_computation | async-start | bytes 56623104 | tf_op jit(solution)/shard_map/psum | solution.py:14
  7.7 66.9 %copy-start.10 = (s32[512,512]{1,0:T(8,128)}, s32[512,512]{1,0:T(8,128)S(1)}, u32[]{:S(2)}) copy-start(s32[512,512]{1,0:T(8,128)S(1)} %fusion.93) | copy-start | bytes 3145732
  12.5 42.9 %copy-start.27 = (f32[2048]{0:T(1024)}, f32[2048]{0:T(1024)S(1)}, u32[]{:S(2)}) copy-start(f32[2048]{0:T(1024)S(1)} %get-tuple-element.306) | copy-start | bytes 24580
  25.4 10.7 copy-start.34
  25.4 10.7 copy-start.52
  31.6 4.5 copy-start.4
  51.0 4.4 copy-start.5
  64.1 10.5 copy-start.36
  167.7 5.6 copy-start.25
  167.7 5.6 copy-start.6
  167.7 5.6 copy-start.49
  172.2 7.1 slice-start.7
  173.3 6.0 copy-start.46
  173.3 6.0 slice-start.8
  193.1 19.2 %copy-start.29 = (f32[768]{0:T(1024)S(1)}, f32[768]{0:T(1024)}, u32[]{:S(2)}) copy-start(f32[768]{0:T(1024)} %param.31) | copy-start | bytes 9220
  193.1 19.2 %copy-start.31 = (f32[4,512]{1,0:T(4,128)S(1)}, f32[4,512]{1,0:T(4,128)}, u32[]{:S(2)}) copy-start(f32[4,512]{1,0:T(4,128)} %get-tuple-element.312) | copy-start | bytes 24580
  212.3 76.4 %copy-start.48 = (s32[64]{0:T(128)S(1)}, s32[64]{0:T(128)}, u32[]{:S(2)}) copy-start(s32[64]{0:T(128)} %param.21) | copy-start | bytes 772
  212.3 78.2 %copy-start.32 = (f32[1,4,4,128]{3,2,1,0:T(4,128)S(1)}, f32[1,4,4,128]{3,2,1,0:T(4,128)}, u32[]{:S(2)}) copy-start(f32[1,4,4,128]{3,2,1,0:T(4,128)} %get-tuple-element.311) | copy-start | bytes 24580
  288.6 7.1 copy-start.37
  288.6 7.1 copy-start.39
  290.4 5.3 copy-start.41
  295.7 44.2 %slice-start.5 = ((s8[6291456]{0:T(1024)(128)(4,1)}), s8[4194304]{0:T(1024)(128)(4,1)S(1)}, s32[]{:S(2)}) async-start(s8[6291456]{0:T(1024)(128)(4,1)} %bitcast.253), calls=%async_computation.7 | async-start | bytes 8388608
  300.6 39.2 %slice-start.6 = ((s8[6291456]{0:T(1024)(128)(4,1)}), s8[2097152]{0:T(1024)(128)(4,1)S(1)}, s32[]{:S(2)}) async-start(s8[6291456]{0:T(1024)(128)(4,1)} %bitcast.253), calls=%async_computation.8 | async-start | bytes 4194304
  318.9 54.0 %slice-start = ((s8[6291456]{0:T(1024)(128)(4,1)}), s8[2097152]{0:T(1024)(128)(4,1)S(1)}, s32[]{:S(2)}) async-start(s8[6291456]{0:T(1024)(128)(4,1)} %bitcast.243), calls=%async_computation.2 | async-start | bytes 4194304
  339.9 33.0 %slice-start.1 = ((s8[6291456]{0:T(1024)(128)(4,1)}), s8[4194304]{0:T(1024)(128)(4,1)S(1)}, s32[]{:S(2)}) async-start(s8[6291456]{0:T(1024)(128)(4,1)} %bitcast.243), calls=%async_computation.3 | async-start | bytes 8388608
  357.3 15.6 %copy-start.17 = (f32[2048,768]{1,0:T(8,128)S(1)}, f32[2048,768]{1,0:T(8,128)}, u32[]{:S(2)}) copy-start(f32[2048,768]{1,0:T(8,128)} %get-tuple-element.322) | copy-start | bytes 18874372
  372.9 3.5 copy-start.19
  376.5 4.1 copy-start.9
  376.5 4.1 copy-start.50
  400.1 6.2 copy-start.26
  407.1 8.8 copy-start.3
  439.9 6.1 copy-start.1
  449.9 8.8 copy-start.3
  486.6 6.1 copy-start.1
  496.7 8.8 copy-start.3
  533.4 6.1 copy-start.1
  543.4 8.8 copy-start.3
  580.2 6.1 copy-start.1
  589.5 5.6 copy-start.7
  589.6 5.6 copy-start.28
  589.6 5.5 copy-start.35
  595.1 4.7 copy-start.14
  595.1 4.6 copy-start.13
  603.2 5.1 copy-start.20
  603.2 5.1 copy-start.12
  618.1 904.7 %all-reduce.9.cloned.1.call-start = ((), (), s32[]{:S(2)}) async-start(), calls=%async_computation.1 | async-start | bytes 56623104 | tf_op jit(solution)/shard_map/psum | solution.py:15
  1366.6 19.3 %copy-start.38 = (f32[64]{0:T(128)S(1)}, f32[64]{0:T(128)}, u32[]{:S(2)}) copy-start(f32[64]{0:T(128)} %copy-done.37) | copy-start | bytes 772
  1366.7 19.3 %copy-start.40 = (f32[64]{0:T(128)S(1)}, f32[64]{0:T(128)}, u32[]{:S(2)}) copy-start(f32[64]{0:T(128)} %copy-done.39) | copy-start | bytes 772
  1366.7 19.3 %copy-start.43 = (f32[64]{0:T(128)S(1)}, f32[64]{0:T(128)}, u32[]{:S(2)}) copy-start(f32[64]{0:T(128)} %copy-done.42) | copy-start | bytes 772
  1366.7 19.3 %copy-start.45 = (f32[64]{0:T(128)S(1)}, f32[64]{0:T(128)}, u32[]{:S(2)}) copy-start(f32[64]{0:T(128)} %copy-done.44) | copy-start | bytes 772
  1366.7 21.8 %copy-start.51 = (bf16[768,768]{1,0:T(8,128)(2,1)S(1)}, bf16[768,768]{1,0:T(8,128)(2,1)}, u32[]{:S(2)}) copy-start(bf16[768,768]{1,0:T(8,128)(2,1)} %param.23) | copy-start | bytes 3538948
  1388.5 19.4 %copy-start.2 = (f32[12,512,512]{2,0,1:T(8,128)S(1)}, f32[12,512,512]{2,0,1:T(8,128)}, u32[]{:S(2)}) copy-start(f32[12,512,512]{2,0,1:T(8,128)} %copy.84) | copy-start | bytes 37748740
  1397.7 10.3 copy-start.11
  1407.9 17.5 %copy-start.8 = (bf16[1,2048,768]{2,1,0:T(8,128)(2,1)S(1)}, bf16[1,2048,768]{2,1,0:T(8,128)(2,1)}, u32[]{:S(2)}) copy-start(bf16[1,2048,768]{2,1,0:T(8,128)(2,1)} %param.18) | copy-start | bytes 9437188
  1407.9 17.5 %copy-start.15 = (bf16[96,8,4,512]{3,1,2,0:T(8,128)(2,1)S(1)}, bf16[96,8,4,512]{3,1,2,0:T(8,128)(2,1)}, u32[]{:S(2)}) copy-start(bf16[96,8,4,512]{3,1,2,0:T(8,128)(2,1)} %copy-done.14) | copy-start | bytes 9437188
  1425.5 10.2 copy-start.33
  1425.5 10.2 copy-start.47
  1425.5 89.2 %copy-start.30 = (f32[2048]{0:T(1024)S(1)}, f32[2048]{0:T(1024)}, u32[]{:S(2)}) copy-start(f32[2048]{0:T(1024)} %get-tuple-element.305) | copy-start | bytes 24580
  1522.9 4.8 copy-start.23
  1522.9 6.2 copy-start.22
  1529.1 10.7 slice-start.2
  1530.5 9.3 slice-start.3
  1530.5 9.3 slice-start.4
  (6 other events, 12.2 us)
Sparse Core Ops, SparseCore 0:
  618.2 748.3 all-reduce.6
  1370.1 90.4 all-reduce.8
